TPU v7x, 32 devices: a whole 2x2x4 slice. The times are simulated.
32 devices in a mesh: ctx: 8 (over y, x, core), ch: 4 (over z).
Axes of the slice: x: 2, y: 2, z: 4, core: 2. Of those that a mesh axis runs over, the one named last changes fastest.
Arguments:
- query_act: bfloat16 [4096, 4096], P('ctx', 'ch'), may hold values from -6 to 6
- key_act: bfloat16 [4096, 4096], P('ctx', 'ch'), may hold values from -6 to 6
- value_act: bfloat16 [4096, 4096], P('ctx', 'ch'), may hold values from -6 to 6
- filters: bfloat16 [4096, 128], P('ch'), may hold values from -0.5 to 0.5
- proj_weight: bfloat16 [8192, 4096], P('ctx', 'ch'), may hold values from -0.09375 to 0.09375
- cotangent: bfloat16 [4096, 8192], P('ctx', 'ch'), may hold values from -6 to 6
Outputs:
- grad_query: bfloat16 [4096, 4096], P('ctx', 'ch')
- grad_key: bfloat16 [4096, 4096], P('ctx', 'ch')
- grad_value: bfloat16 [4096, 4096], P('ctx', 'ch')
- grad_filter: float32 [4096, 128], P('ch')
- grad_proj: float32 [8192, 4096], P('ctx', 'ch')
All inputs are finite; a program needn't handle non-finite values.
Results may differ from a plain program's by a relative error of at most 0.0051.
Values may be sent and summed in bfloat16 or wider, within the bound.
A program may use at most 192 MiB of HBM per device.

v0:
```python
import jax
import jax.numpy as jnp
import numpy as np
from jax import lax
from jax.sharding import PartitionSpec as P

TAPS = 128


def from_behind(x, axis, by):
    length = lax.axis_size(axis)
    pairs = [(i, i + by) for i in range(length) if 0 <= i + by < length]
    return lax.ppermute(x, axis, pairs)


def basis(points):
    freqs = points // 2
    phase = (2 * np.arange(freqs)[:, None] + 1) * np.arange(points)[None, :] % (2 * points)
    angle = np.pi * phase / points
    return np.concatenate([np.cos(angle), np.sin(angle)], 0).astype(np.float32)


def split(a):
    a = jnp.asarray(a, jnp.float32)
    hi = a.astype(jnp.bfloat16)
    return (hi, (a - hi.astype(jnp.float32)).astype(jnp.bfloat16))


def dot32(a, b):
    return jnp.dot(a, b, preferred_element_type=jnp.float32)


def forward(table, x):
    hi, lo = split(table)
    return dot32(hi, x) + dot32(lo, x)


def backward(table, y):
    thi, tlo = split(table)
    yhi, ylo = split(y)
    return dot32(thi, yhi) + dot32(thi, ylo) + dot32(tlo, yhi)


def halves(x):
    n = x.shape[0] // 2
    return (x[:n], x[n:])


def times(x, f):
    (xc, xs), (fc, fs) = (halves(x), halves(f))
    return jnp.concatenate([xc * fc - xs * fs, xc * fs + xs * fc], 0)


def times_conj(x, f):
    (xc, xs), (fc, fs) = (halves(x), halves(f))
    return jnp.concatenate([xc * fc + xs * fs, xs * fc - xc * fs], 0)


def shards(query_act, key_act, value_act, filters, proj_weight, cotangent):
    tokens = query_act.shape[0]
    points = tokens + TAPS
    table = basis(points)
    inverse = (table.T / (points // 2)).astype(np.float32)
    gathered = lax.all_gather(cotangent, "ch", axis=1, tiled=True)
    weight = lax.all_gather(proj_weight, "ctx", axis=0, tiled=True)
    query_f = query_act.astype(jnp.float32)
    key_f = key_act.astype(jnp.float32)
    value_f = value_act.astype(jnp.float32)
    product = (key_f * value_f).astype(jnp.bfloat16)
    before = from_behind(product[tokens - TAPS :], "ctx", 1)
    filt_spec = forward(table[:, :TAPS], filters.T)
    prod_spec = forward(table[:, :TAPS], before) + forward(table[:, TAPS:], product)
    mixed = backward(inverse[TAPS:], times(prod_spec, filt_spec))
    gated = (query_f * mixed).astype(jnp.bfloat16)
    partial_grad = lax.dot_general(
        gathered, gated, (((0,), (0,)), ((), ())), preferred_element_type=jnp.float32
    ).astype(jnp.bfloat16)
    grad_proj = lax.psum_scatter(partial_grad, "ctx", scatter_dimension=0, tiled=True).astype(
        jnp.float32
    )
    grad_mix = dot32(gathered, weight)
    grad_query = (grad_mix * mixed).astype(jnp.bfloat16)
    grad_gate = (grad_mix * query_f).astype(jnp.bfloat16)
    after = from_behind(grad_gate[:TAPS], "ctx", -1)
    own_spec = forward(table[:, :tokens], grad_gate)
    gate_spec = own_spec + forward(table[:, tokens:], after)
    lags = inverse[TAPS - np.arange(TAPS)]
    local_filter = backward(lags, times_conj(prod_spec, own_spec))
    grad_filter = lax.psum(local_filter, "ctx").T
    grad_prod = backward(inverse[:tokens], times_conj(gate_spec, filt_spec))
    grad_key = (grad_prod * value_f).astype(jnp.bfloat16)
    grad_value = (grad_prod * key_f).astype(jnp.bfloat16)
    return (grad_query, grad_key, grad_value, grad_filter, grad_proj)


def solution(mesh):
    return jax.shard_map(
        shards,
        mesh=mesh,
        in_specs=(
            P("ctx", "ch"),
            P("ctx", "ch"),
            P("ctx", "ch"),
            P("ch", None),
            P("ctx", "ch"),
            P("ctx", "ch"),
        ),
        out_specs=(P("ctx", "ch"), P("ctx", "ch"), P("ctx", "ch"), P("ch", None), P("ctx", "ch")),
        check_vma=False,
    )
```

profile of v0, /device:TPU:0, one launch (start us, length us, event | category | flops | bytes accessed | tf_op | source)
XLA Modules:
  0.0 497.0 jit_solution(8108205557831197759)
XLA Ops:
  7.2 0.0 copy-start
  7.2 0.0 all-gather.3.cloned.1.call-start
  7.2 0.7 all-gather.3.cloned.1.call-update
  7.9 0.0 all-gather.5.cloned.1.call-start
  8.0 0.7 all-gather.5.cloned.1.call-update
  8.7 0.0 copy-start.20
  8.7 0.0 reduce-scatter.2.cloned.1.call-start
  8.8 1.3 copy.19
  10.1 1.3 copy.20
  11.4 0.5 fusion.39
  11.9 0.5 convolution_add_fusion
  12.4 149.5 %all-gather.3.cloned.1.call-done = bf16[512,8192]{1,0:T(8,128)(2,1)} async-done(((bf16[512,2048]{1,0:T(8,128)(2,1)}), bf16[512,8192]{1,0:T(8,128)(2,1)}) %all-gather.3.cloned.1.call-update) | async-done | bytes 8388624 | tf_op jit(solution)/shard_map/all_gather | solution.py:64
  162.0 90.0 %all-gather.5.cloned.1.call-done = bf16[8192,1024]{1,0:T(8,128)(2,1)} async-done(((bf16[1024,1024]{1,0:T(8,128)(2,1)}), bf16[8192,1024]{1,0:T(8,128)(2,1)}) %all-gather.5.cloned.1.call-update) | async-done | bytes 16777232 | tf_op jit(solution)/shard_map/all_gather | solution.py:65
  251.9 14.9 %fusion.6 = (bf16[512,1024]{1,0:T(8,128)(2,1)S(1)}, f32[512,1024]{1,0:T(8,128)S(1)}) fusion(bf16[512,1024]{1,0:T(8,128)(2,1)} %param.14, bf16[512,8192]{1,0:T(8,128)(2,1)} %all-gather.3.cloned.1.call-done, bf16[8192,1024]{1,0:T(8,128)(2,1)} %all-gather.5.cloned.1.call-done), kind=kOutput, calls=%fused_computation.20 | convolution fusion | flops 8591507456 | bytes 29360128 | tf_op jit(solution)/shard_map/dot_general | solution.py:30
  266.9 0.0 copy-start.18
  266.9 1.4 collective-permute-start.1
  268.4 0.9 fusion.40
  269.2 0.0 copy-start.22
  269.2 0.9 convolution_add_fusion.1
  270.1 0.0 copy-start.24
  270.1 0.4 collective-permute-done.1
  270.5 0.5 fusion.41
  271.0 0.1 copy-done.24
  271.0 0.5 add_add_fusion
  271.5 0.6 multiply_add_fusion.1
  272.2 0.5 copy-done.8
  272.6 1.0 fusion.8
  273.7 0.0 copy-start.12
  273.7 1.0 fusion.21
  274.7 0.2 copy-done.5
  274.9 0.3 copy-done.6
  275.2 0.2 copy-done.12
  275.4 2.7 fusion.3
  278.1 0.0 copy-start.16
  278.1 6.7 %collective-permute-start = (bf16[128,1024]{0,1:T(8,128)(2,1)S(1)}, bf16[128,1024]{0,1:T(8,128)(2,1)S(1)}, u32[]{:S(2)}, u32[]{:S(2)}) collective-permute-start(bf16[128,1024]{0,1:T(8,128)(2,1)S(1)} %slice.44), channel_id=1, source_target_pairs={{0,4},{4,8},{8,12},{12,16},{16,20},{20,24},{24,28},{1,5},{5,9},{9,... | collective-permute-start | bytes 786440 | tf_op jit(solution)/shard_map/ppermute | solution.py:13
  284.8 0.9 fusion.38
  285.7 0.0 copy-start.14
  285.7 0.9 fusion.37
  286.6 0.0 copy-start.21
  286.6 0.5 fusion.36
  287.1 0.4 copy-done.21
  287.5 0.7 add_add_fusion.1
  288.2 0.0 copy-start.15
  288.2 2.5 multiply_add_fusion
  290.7 1.0 fusion.14
  291.7 0.1 copy-done.7
  291.8 1.0 fusion.17
  292.8 2.1 multiply_convert_fusion
  294.9 15.9 %convert_bitcast_fusion = bf16[8192,1024]{0,1:T(8,128)(2,1)} fusion(bf16[512,8192]{1,0:T(8,128)(2,1)} %all-gather.3.cloned.1.call-done, f32[512,1024]{1,0:T(8,128)S(1)} %get-tuple-element.24, bf16[512,1024]{1,0:T(8,128)(2,1)S(1)} %copy-done.25), kind=kOutput, calls=%fused_computation | convolution fusion | flops 8599896064 | bytes 28311552 | tf_op jit(solution)/shard_map/dot_general | solution.py:75
  310.7 0.0 reduce-scatter.2.cloned.1.call-update
  310.8 0.3 all-reduce.2.cloned.1.call-start
  311.0 1.0 copy-done.2
  312.0 0.4 copy-done.3
  312.4 0.5 fusion.25
  313.0 0.5 fusion.11
  313.6 0.4 copy-done.23
  313.9 1.4 fusion.12
  315.3 0.0 all-reduce.2.cloned.1.call-update
  315.4 2.4 copy.26
  317.7 1.3 copy.25
  319.0 111.5 %reduce-scatter.2.cloned.1.call-done = bf16[1024,1024]{0,1:T(8,128)(2,1)} async-done(((bf16[8192,1024]{0,1:T(8,128)(2,1)}), bf16[1024,1024]{0,1:T(8,128)(2,1)}) %reduce-scatter.2.cloned.1.call-update) | async-done | bytes 2097168 | tf_op jit(solution)/shard_map/reduce_scatter | solution.py:78
  430.5 4.2 copy.27
  434.6 53.9 %all-reduce.2.cloned.1.call-done = f32[1024,128]{1,0:T(8,128)} async-done(((f32[1024,128]{1,0:T(8,128)}), f32[1024,128]{1,0:T(8,128)}) %all-reduce.2.cloned.1.call-update) | async-done | bytes 524304 | tf_op jit(solution)/shard_map/psum | solution.py:89
  488.6 1.9 copy.33
  (35 shorter events, 0.1 us)
Async XLA Ops:
  7.2 4.2 copy-start
  7.2 1.6 copy-start.10
  7.2 154.8 %all-gather.3.cloned.1.call-start = ((), (), s32[]{:S(2)}) async-start(), calls=%async_computation.1 | async-start | bytes 10485760 | tf_op jit(solution)/shard_map/all_gather | solution.py:64
  7.9 2.2 copy-start.11
  7.9 244.0 %all-gather.5.cloned.1.call-start = ((), (), s32[]{:S(2)}) async-start(), calls=%async_computation.2 | async-start | bytes 18874368 | tf_op jit(solution)/shard_map/all_gather | solution.py:65
  8.7 2.7 copy-start.20
  8.7 421.8 %reduce-scatter.2.cloned.1.call-start = ((), (), s32[]{:S(2)}) async-start(), calls=%async_computation.4 | async-start | bytes 18874368 | tf_op jit(solution)/shard_map/reduce_scatter | solution.py:78
  10.1 1.8 copy-start.13
  12.4 255.9 %copy-start.9 = (bf16[640,512]{1,0:T(8,128)(2,1)S(1)}, bf16[640,512]{1,0:T(8,128)(2,1)}, u32[]{:S(2)}) copy-start(bf16[640,512]{1,0:T(8,128)(2,1)} %constant.33) | copy-start | bytes 1966084
  266.9 2.3 copy-start.18
  266.9 3.6 collective-permute-start.1
  269.2 1.2 copy-start.22
  270.1 0.9 copy-start.24
  271.5 1.1 copy-start.8
  273.7 1.2 copy-start.5
  273.7 1.5 copy-start.6
  273.7 1.7 copy-start.12
  275.4 9.4 %copy-start.17 = (bf16[640,512]{1,0:T(8,128)(2,1)S(1)}, bf16[640,512]{1,0:T(8,128)(2,1)}, u32[]{:S(2)}) copy-start(bf16[640,512]{1,0:T(8,128)(2,1)} %constant.28) | copy-start | bytes 1966084
  278.1 7.6 %copy-start.16 = (bf16[640,512]{1,0:T(8,128)(2,1)S(1)}, bf16[640,512]{1,0:T(8,128)(2,1)}, u32[]{:S(2)}) copy-start(bf16[640,512]{1,0:T(8,128)(2,1)} %constant.25) | copy-start | bytes 1966084
  278.1 8.5 %collective-permute-start = (bf16[128,1024]{0,1:T(8,128)(2,1)S(1)}, bf16[128,1024]{0,1:T(8,128)(2,1)S(1)}, u32[]{:S(2)}, u32[]{:S(2)}) collective-permute-start(bf16[128,1024]{0,1:T(8,128)(2,1)S(1)} %slice.44), channel_id=1, source_target_pairs={{0,4},{4,8},{8,12},{12,16},{16,20},{20,24},{24,28},{1,5},{5,9},{9,... | collective-permute-start | bytes 786440 | tf_op jit(solution)/shard_map/ppermute | solution.py:13
  285.7 0.9 copy-start.14
  286.6 0.9 copy-start.21
  288.2 2.5 copy-start.15
  290.7 1.1 copy-start.7
  292.7 2.1 copy-start.25
  310.7 1.3 copy-start.2
  310.7 1.7 copy-start.3
  310.7 1.7 copy-start.19
  310.8 177.8 %all-reduce.2.cloned.1.call-start = ((), (), s32[]{:S(2)}) async-start(), calls=%async_computation.3 | async-start | bytes 1048576 | tf_op jit(solution)/shard_map/psum | solution.py:89
  313.0 0.9 copy-start.23
  315.3 2.4 copy-start.4
  430.5 60.0 %copy-start.1 = (bf16[1024,128]{1,0:T(8,128)(2,1)S(1)}, bf16[1024,128]{1,0:T(8,128)(2,1)}, u32[]{:S(2)}) copy-start(bf16[1024,128]{1,0:T(8,128)(2,1)} %param.17) | copy-start | bytes 786436
Sparse Core Ops, SparseCore 0:
  9.6 152.3 all-gather.2
  163.9 88.0 all-gather.4
  310.9 119.5 reduce-scatter.1
  434.0 54.5 all-reduce.1
where the time goes:
time: 498 us; the launch traced here: 497 us
  waiting for transfers between devices  407 us (82%)
  matrix products  48.7 us (10%)
  local copies, waits for them, and re-layouts  15.9 us (3%)
  between operations  14.1 us (3%)
  starting transfers between devices  8.5 us (2%)
    all_gather x1, waiting for transfers between devices, shards(): gathered = lax.all_gather(cotangent, 'ch', axis=1, tiled=True)  150 us
    reduce_scatter x1, waiting for transfers between devices, shards(): lax.psum_scatter(partial_grad, 'ctx', scatter_dimension=0, tiled=True)  111 us
    all_gather x1, waiting for transfers between devices, shards(): weight = lax.all_gather(proj_weight, 'ctx', axis=0, tiled=True)  90 us
    psum x1, waiting for transfers between devices, shards(): grad_filter = lax.psum(local_filter, 'ctx').T  53.9 us
    dot_general x20, matrix products, dot32(): return jnp.dot(a, b, preferred_element_type=jnp.float32)  32.9 us
    dot_general x1, matrix products, shards(): lax.dot_general(gathered, gated, (((0,), (0,)), ((), ())), preferred_elem...  15.9 us
    unnamed x58, local copies, waits for them, and re-layouts  15.9 us
  transfers between devices with their start and end apart: 6, of which 5 were waited for; matrix products, arithmetic and copies ran while one was open for 4% of the time, Pallas kernels for 0%

commit v1 on v0

--- a/solution.py
+++ b/solution.py
@@ -5,6 +5,20 @@
 from jax.sharding import PartitionSpec as P
 
 TAPS = 128
+
+
+def use_paths(t0, across):
+    local_now, carry = (lax.axis_size(across), lax.axis_index(across))
+    reply, lower = (t0, 1)
+    while lower < local_now:
+        built = lax.ppermute(
+            reply, across, list(map(lambda nth: (nth, nth ^ lower), range(local_now)))
+        )
+        block_out = jnp.concatenate([reply, built], axis=0)
+        met_up = jnp.concatenate([built, reply], axis=0)
+        reply = jnp.where(carry & lower == 0, block_out, met_up)
+        lower = 2 * lower
+    return reply
 
 
 def from_behind(x, axis, by):
@@ -62,7 +76,7 @@
     table = basis(points)
     inverse = (table.T / (points // 2)).astype(np.float32)
     gathered = lax.all_gather(cotangent, "ch", axis=1, tiled=True)
-    weight = lax.all_gather(proj_weight, "ctx", axis=0, tiled=True)
+    weight = use_paths(proj_weight, "ctx")
     query_f = query_act.astype(jnp.float32)
     key_f = key_act.astype(jnp.float32)
     value_f = value_act.astype(jnp.float32)

time: 498 us -> 555 us (1.11)
  waiting for transfers between devices: 407 us -> 437 us
  other arithmetic: 3.06 us -> 17.8 us
    ppermute x0 -> x3, waiting for transfers between devices: none -> 229 us  [use_paths(): lax.ppermute(reply, across, list(map(lambda nth: (nth, nth ^ lower), rang...]
    all_gather x1, waiting for transfers between devices: 150 us -> 42.1 us  [shards(): gathered = lax.all_gather(cotangent, 'ch', axis=1, tiled=True)]
    all_gather x1 -> x0, waiting for transfers between devices: 90 us -> none  [shards(): weight = lax.all_gather(proj_weight, 'ctx', axis=0, tiled=True)]
    select_n x0 -> x2, other arithmetic: none -> 14.7 us  [use_paths(): reply = jnp.where(carry & lower == 0, block_out, met_up)]
    unnamed x58 -> x62, local copies, waits for them, and re-layouts: 15.9 us -> 18.9 us
  transfers between devices with their start and end apart: 6 -> 8, of which waited for: 5 -> 7; matrix products, arithmetic and copies ran while one was open for 4% -> 5% of each run, Pallas kernels for 0% -> 0%
where the time goes in v1:
time: 555 us
  waiting for transfers between devices  437 us (79%)
  matrix products  53.2 us (10%)
  local copies, waits for them, and re-layouts  19.9 us (4%)
  other arithmetic  17.8 us (3%)
  between operations  14.1 us (3%)
  starting transfers between devices  13.1 us (2%)
    ppermute x3, waiting for transfers between devices, use_paths(): lax.ppermute(reply, across, list(map(lambda nth: (nth, nth ^ lower), rang...  229 us
    reduce_scatter x1, waiting for transfers between devices, shards(): lax.psum_scatter(partial_grad, 'ctx', scatter_dimension=0, tiled=True)  111 us
    psum x1, waiting for transfers between devices, shards(): grad_filter = lax.psum(local_filter, 'ctx').T  54.1 us
    all_gather x1, waiting for transfers between devices, shards(): gathered = lax.all_gather(cotangent, 'ch', axis=1, tiled=True)  42.1 us
    dot_general x20, matrix products, dot32(): return jnp.dot(a, b, preferred_element_type=jnp.float32)  38.2 us
    unnamed x62, local copies, waits for them, and re-layouts  18.9 us
    dot_general x1, matrix products, shards(): lax.dot_general(gathered, gated, (((0,), (0,)), ((), ())), preferred_elem...  15.1 us
    select_n x2, other arithmetic, use_paths(): reply = jnp.where(carry & lower == 0, block_out, met_up)  14.7 us
  transfers between devices with their start and end apart: 8, of which 7 were waited for; matrix products, arithmetic and copies ran while one was open for 5% of the time, Pallas kernels for 0%

profile of v1, /device:TPU:0, one launch (start us, length us, event | category | flops | bytes accessed | tf_op | source)
XLA Modules:
  0.0 554.8 jit_solution(6287772724912127776)
XLA Ops:
  7.2 0.0 copy-start
  7.2 0.0 all-gather.2.cloned.1.call-start
  7.2 0.5 collective-permute-start
  7.7 4.0 collective-permute-done
  11.7 4.7 maximum_select_fusion.3
  16.5 2.9 collective-permute-start.1
  19.3 0.0 all-gather.2.cloned.1.call-update
  19.3 0.0 reduce-scatter.2.cloned.1.call-start
  19.4 91.1 %collective-permute-done.1 = bf16[2048,1024]{1,0:T(8,128)(2,1)} collective-permute-done((bf16[2048,1024]{1,0:T(8,128)(2,1)}, bf16[2048,1024]{1,0:T(8,128)(2,1)}, u32[]{:S(2)}, u32[]{:S(2)}) %collective-permute-start.1) | collective-permute-done | bytes 4194336 | tf_op jit(solution)/shard_map/ppermute | solution.py:14
  110.5 10.0 %maximum_select_fusion.2 = bf16[4096,1024]{1,0:T(8,128)(2,1)} fusion(bf16[2048,1024]{1,0:T(8,128)(2,1)} %collective-permute-done.1, bf16[2048,1024]{1,0:T(8,128)(2,1)} %maximum_select_fusion.3, pred[]{:T(512)S(6)} %eq.10), kind=kLoop, calls=%fused_computation.9 | loop fusion | flops 37748736 | bytes 16777216 | tf_op jit(solution)/shard_map/jit(_where)/select_n | solution.py:19
  120.5 1.8 collective-permute-start.2
  122.4 1.3 copy.22
  123.7 1.3 copy.19
  125.0 1.3 copy.20
  126.3 0.5 fusion.48
  126.9 0.5 convolution_add_fusion
  127.4 42.1 %all-gather.2.cloned.1.call-done = bf16[512,8192]{1,0:T(8,128)(2,1)} async-done(((bf16[512,2048]{1,0:T(8,128)(2,1)}), bf16[512,8192]{1,0:T(8,128)(2,1)}) %all-gather.2.cloned.1.call-update) | async-done | bytes 8388624 | tf_op jit(solution)/shard_map/all_gather | solution.py:78
  169.5 133.5 %collective-permute-done.2 = bf16[4096,1024]{1,0:T(8,128)(2,1)} collective-permute-done((bf16[4096,1024]{1,0:T(8,128)(2,1)}, bf16[4096,1024]{1,0:T(8,128)(2,1)}, u32[]{:S(2)}, u32[]{:S(2)}) %collective-permute-start.2) | collective-permute-done | bytes 8388640 | tf_op jit(solution)/shard_map/ppermute | solution.py:14
  302.9 18.6 %fusion.13 = (bf16[512,1024]{0,1:T(8,128)(2,1)}, f32[1024,512]{1,0:T(8,128)}) fusion(bf16[512,1024]{0,1:T(8,128)(2,1)} %copy.22, bf16[512,8192]{1,0:T(8,128)(2,1)} %all-gather.2.cloned.1.call-done, bf16[4096,1024]{1,0:T(8,128)(2,1)} %collective-permute-done.2, bf16[4096,1024]{1,0:T(8,128)(2,1)} %maximum_select_fusion.2, pred[]{:T(512)S(6)} %eq.9), kind=kOutput, calls=%fused_computation.30 | convolution fusion | flops 8667004928 | bytes 29360128 | tf_op jit(solution)/shard_map/dot_general | solution.py:44
  321.5 1.0 slice.49
  322.5 2.4 fusion.49
  324.9 1.6 collective-permute-start.4
  326.5 0.9 convolution_add_fusion.1
  327.4 1.0 collective-permute-done.4
  328.5 0.5 fusion.50
  329.0 0.5 add_add_fusion
  329.5 0.0 copy-start.10
  329.5 0.6 multiply_add_fusion.1
  330.2 0.5 copy-done.10
  330.6 1.0 fusion.29
  331.7 1.0 fusion.17
  332.7 0.2 copy-done.6
  332.9 0.3 copy-done.7
  333.2 0.2 copy-done.17
  333.4 2.8 fusion.10
  336.2 0.9 fusion.46
  337.1 6.2 %collective-permute-start.3 = (bf16[128,1024]{0,1:T(8,128)(2,1)S(1)}, bf16[128,1024]{0,1:T(8,128)(2,1)S(1)}, u32[]{:S(2)}, u32[]{:S(2)}) collective-permute-start(bf16[128,1024]{0,1:T(8,128)(2,1)S(1)} %slice.44), channel_id=1, source_target_pairs={{0,4},{4,8},{8,12},{12,16},{16,20},{20,24},{24,28},{1,5},{5,9},{9,... | collective-permute-start | bytes 786440 | tf_op jit(solution)/shard_map/ppermute | solution.py:27
  343.3 0.9 fusion.47
  344.2 0.0 collective-permute-done.3
  344.2 0.5 fusion.45
  344.7 0.6 add_add_fusion.1
  345.3 2.5 multiply_add_fusion
  347.8 1.0 fusion.25
  348.9 1.0 fusion.16
  349.9 0.5 copy-done.11
  350.4 0.1 copy-done.16
  350.6 2.0 fusion.15
  352.6 15.1 %convert_bitcast_fusion = bf16[8192,1024]{0,1:T(8,128)(2,1)} fusion(bf16[512,8192]{1,0:T(8,128)(2,1)} %all-gather.2.cloned.1.call-done, f32[512,1024]{0,1:T(8,128)S(1)} %get-tuple-element.24, bf16[512,1024]{0,1:T(8,128)(2,1)S(1)} %copy-done.15), kind=kOutput, calls=%fused_computation.7 | convolution fusion | flops 8599896064 | bytes 28311552 | tf_op jit(solution)/shard_map/dot_general | solution.py:89
  367.7 0.0 reduce-scatter.2.cloned.1.call-update
  367.7 0.0 all-reduce.2.cloned.1.call-start
  367.8 1.2 copy-done.2
  369.0 0.4 copy-done.3
  369.4 0.5 fusion.33
  370.0 0.6 fusion.20
  370.5 0.3 copy-done.25
  370.9 1.4 fusion.21
  372.3 0.0 all-reduce.2.cloned.1.call-update
  372.3 2.4 copy.26
  374.7 1.3 copy.27
  376.1 1.3 copy.25
  377.4 110.8 %reduce-scatter.2.cloned.1.call-done = bf16[1024,1024]{0,1:T(8,128)(2,1)} async-done(((bf16[8192,1024]{0,1:T(8,128)(2,1)}), bf16[1024,1024]{0,1:T(8,128)(2,1)}) %reduce-scatter.2.cloned.1.call-update) | async-done | bytes 2097168 | tf_op jit(solution)/shard_map/reduce_scatter | solution.py:92
  488.1 4.2 copy.28
  492.3 54.1 %all-reduce.2.cloned.1.call-done = f32[1024,128]{1,0:T(8,128)} async-done(((f32[1024,128]{1,0:T(8,128)}), f32[1024,128]{1,0:T(8,128)}) %all-reduce.2.cloned.1.call-update) | async-done | bytes 524304 | tf_op jit(solution)/shard_map/psum | solution.py:103
  546.4 1.9 copy.33
  (44 shorter events, 0.2 us)
Async XLA Ops:
  7.2 119.2 %copy-start = (bf16[1024,128]{1,0:T(8,128)(2,1)S(1)}, bf16[1024,128]{1,0:T(8,128)(2,1)}, u32[]{:S(2)}) copy-start(bf16[1024,128]{1,0:T(8,128)(2,1)} %param.17) | copy-start | bytes 786436
  7.2 162.3 %all-gather.2.cloned.1.call-start = ((), (), s32[]{:S(2)}) async-start(), calls=%async_computation.1 | async-start | bytes 10485760 | tf_op jit(solution)/shard_map/all_gather | solution.py:78
  7.2 4.5 collective-permute-start
  16.5 94.0 %collective-permute-start.1 = (bf16[2048,1024]{1,0:T(8,128)(2,1)}, bf16[2048,1024]{1,0:T(8,128)(2,1)}, u32[]{:S(2)}, u32[]{:S(2)}) collective-permute-start(bf16[2048,1024]{1,0:T(8,128)(2,1)} %maximum_select_fusion.3), channel_id=1, source_target_pairs={{0,8},{4,12},{8,0},{12,4},{16,24},{20,28},{24,16},{28,20},{1,9},{5... | collective-permute-start | bytes 12582920 | tf_op jit(solution)/shard_map/ppermute | solution.py:14
  19.3 468.8 %reduce-scatter.2.cloned.1.call-start = ((), (), s32[]{:S(2)}) async-start(), calls=%async_computation.3 | async-start | bytes 18874368 | tf_op jit(solution)/shard_map/reduce_scatter | solution.py:92
  19.4 103.0 %copy-start.12 = (bf16[512,1024]{1,0:T(8,128)(2,1)S(1)}, bf16[512,1024]{1,0:T(8,128)(2,1)}, u32[]{:S(2)}) copy-start(bf16[512,1024]{1,0:T(8,128)(2,1)} %param.14) | copy-start | bytes 3145732
  120.5 3.2 copy-start.13
  120.5 4.5 copy-start.14
  120.5 182.4 %collective-permute-start.2 = (bf16[4096,1024]{1,0:T(8,128)(2,1)}, bf16[4096,1024]{1,0:T(8,128)(2,1)}, u32[]{:S(2)}, u32[]{:S(2)}) collective-permute-start(bf16[4096,1024]{1,0:T(8,128)(2,1)} %maximum_select_fusion.2), channel_id=1, source_target_pairs={{0,16},{4,20},{8,24},{12,28},{16,0},{20,4},{24,8},{28,12},{1,17},{... | collective-permute-start | bytes 25165832 | tf_op jit(solution)/shard_map/ppermute | solution.py:14
  123.7 2.6 copy-start.23
  125.0 1.8 copy-start.18
  322.4 4.1 copy-start.4
  322.4 4.1 copy-start.21
  324.9 3.6 copy-start.24
  324.9 3.6 collective-permute-start.4
  327.4 1.6 copy-start.26
  329.5 1.1 copy-start.10
  331.6 1.2 copy-start.6
  331.7 1.5 copy-start.7
  331.7 1.7 copy-start.17
  333.4 2.8 copy-start.20
  336.2 7.1 %copy-start.19 = (bf16[640,512]{1,0:T(8,128)(2,1)S(1)}, bf16[640,512]{1,0:T(8,128)(2,1)}, u32[]{:S(2)}) copy-start(bf16[640,512]{1,0:T(8,128)(2,1)} %constant.42) | copy-start | bytes 1966084
  337.1 7.1 %collective-permute-start.3 = (bf16[128,1024]{0,1:T(8,128)(2,1)S(1)}, bf16[128,1024]{0,1:T(8,128)(2,1)S(1)}, u32[]{:S(2)}, u32[]{:S(2)}) collective-permute-start(bf16[128,1024]{0,1:T(8,128)(2,1)S(1)} %slice.44), channel_id=1, source_target_pairs={{0,4},{4,8},{8,12},{12,16},{16,20},{20,24},{24,28},{1,5},{5,9},{9,... | collective-permute-start | bytes 786440 | tf_op jit(solution)/shard_map/ppermute | solution.py:27
  345.3 2.5 copy-start.9
  348.9 1.6 copy-start.11
  348.9 1.7 copy-start.16
  350.6 2.0 copy-start.15
  367.7 1.3 copy-start.2
  367.7 1.7 copy-start.3
  367.7 1.7 copy-start.22
  367.7 178.6 %all-reduce.2.cloned.1.call-start = ((), (), s32[]{:S(2)}) async-start(), calls=%async_computation.2 | async-start | bytes 1048576 | tf_op jit(solution)/shard_map/psum | solution.py:103
  370.0 0.9 copy-start.25
  372.3 2.5 copy-start.5
  372.3 3.7 copy-start.8
  488.1 60.1 %copy-start.1 = (bf16[1024,128]{1,0:T(8,128)(2,1)S(1)}, bf16[1024,128]{1,0:T(8,128)(2,1)}, u32[]{:S(2)}) copy-start(bf16[1024,128]{1,0:T(8,128)(2,1)} %param.17) | copy-start | bytes 786436
Sparse Core Ops, SparseCore 0:
  19.5 149.9 all-gather.1
  367.8 120.2 reduce-scatter.1
  491.8 54.5 all-reduce.1
